TPU v7x, 256 devices: a whole 4x4x8 slice. The times are simulated.
256 devices in a mesh: seq: 32 (over y, z), head: 8 (over x, core).
Axes of the slice: x: 4, y: 4, z: 8, core: 2. Of those that a mesh axis runs over, the one named last changes fastest.
Arguments:
- tokens: bfloat16 [32768, 4096], P('seq'), may hold values from -50 to 50
- norm_gain: float32 [4096], replicated, may hold values from 0.1 to 1.9
- wq: bfloat16 [4096, 4096], P('seq', 'head'), may hold values from -2.34375 to 2.34375
- wk: bfloat16 [4096, 1024], P('seq', 'head'), may hold values from -0.09375 to 0.09375
- wv: bfloat16 [4096, 1024], P('seq', 'head'), may hold values from -0.09375 to 0.09375
- wo: bfloat16 [4096, 4096], P('head', 'seq'), may hold values from -0.1875 to 0.1875
- gate_bias: float32 [32], P('head'), may hold values from -3 to 3
- mem_init: float32 [8, 128, 128], P('head'), may hold values from -32768 to 32768
- norm_init: float32 [8, 128], P('head'), may hold values from 512 to 2048
Outputs:
- attended: bfloat16 [32768, 4096], P('seq', 'head')
All inputs are finite; a program needn't handle non-finite values.
Results may differ from a plain program's by a relative error of at most 0.018.
Values may be sent and summed in bfloat16 or wider, within the bound.
No kernel may reach another device: no remote copies, remote signals or barrier semaphores. Data moves between devices by JAX's collectives and lax.ppermute only.
A program may use at most 128 MiB of HBM per device.

v0:
```python
import math
import jax
import jax.numpy as jnp
from jax import lax
from jax.sharding import PartitionSpec as P

H = 32
KVH = 8
HD = 128
SEG = 512


def from_behind(block, axis, distance):
    devices = range(lax.axis_size(axis))
    route = [(i - distance, i) for i in devices if i - distance in devices]
    return lax.ppermute(block, axis, route)


def feature_map(values_in):
    return jnp.where(values_in > 0, values_in + 1.0, jnp.exp(jnp.minimum(values_in, 0.0)))


def per_device(tokens, norm_gain, wq, wk, wv, wo, gate_bias, mem_init, norm_init):
    highest = lax.Precision.HIGHEST
    widened = tokens.astype(jnp.float32)
    normed = (
        widened * lax.rsqrt(jnp.mean(widened * widened, axis=-1, keepdims=True) + 1e-05) * norm_gain
    ).astype(jnp.bfloat16)
    token_count = normed.shape[0]

    def project(shard_piece):
        return jnp.dot(normed, shard_piece, preferred_element_type=jnp.float32)

    query_wide = project(lax.all_gather(wq, "seq", axis=0, tiled=True))
    key_wide = project(lax.all_gather(wk, "seq", axis=0, tiled=True))
    value_wide = project(lax.all_gather(wv, "seq", axis=0, tiled=True))
    queries = query_wide.astype(jnp.bfloat16)
    keys_all = key_wide.astype(jnp.bfloat16)
    values_all = value_wide.astype(jnp.bfloat16)
    group = H // KVH
    kv_local = wk.shape[1] // HD
    segments = token_count // SEG
    query_seg = queries.reshape(segments, SEG, kv_local, group, HD)
    key_seg = keys_all.reshape(segments, SEG, kv_local, HD)
    value_seg = values_all.reshape(segments, SEG, kv_local, HD)
    key_feats = feature_map(key_seg.astype(jnp.float32))
    delta_mem = jnp.einsum(
        "nski,nskj->nkij", key_feats, value_seg.astype(jnp.float32), precision=highest
    )
    delta_norm = jnp.sum(key_feats, axis=1)
    own_mem = jnp.sum(delta_mem, axis=0)
    own_norm = jnp.sum(delta_norm, axis=0)
    zero_mem = jnp.zeros_like(own_mem)
    zero_norm = jnp.zeros_like(own_norm)

    def pass_along(step_index, carried):
        return (
            from_behind((carried[0] + own_mem).astype(jnp.bfloat16), "seq", 1).astype(jnp.float32),
            from_behind((carried[1] + own_norm).astype(jnp.bfloat16), "seq", 1).astype(jnp.float32),
        )

    carried_mem, carried_norm = lax.fori_loop(
        0, lax.axis_size("seq") - 1, pass_along, (zero_mem, zero_norm)
    )
    inner_mem = jnp.concatenate([zero_mem[None], jnp.cumsum(delta_mem, axis=0)[:-1]], axis=0)
    inner_norm = jnp.concatenate([zero_norm[None], jnp.cumsum(delta_norm, axis=0)[:-1]], axis=0)
    mem_before = mem_init[None] + carried_mem[None] + inner_mem
    norm_before = norm_init[None] + carried_norm[None] + inner_norm
    query_feats = feature_map(query_seg.astype(jnp.float32))
    numer = jnp.einsum("nskgi,nkij->nskgj", query_feats, mem_before, precision=highest)
    denom = jnp.einsum("nskgi,nki->nskg", query_feats, norm_before, precision=highest)
    retrieved = numer / denom[..., None]
    score_scale = 1.0 / math.sqrt(HD)
    causal = lax.broadcasted_iota(jnp.int32, (SEG, SEG), 0) >= lax.broadcasted_iota(
        jnp.int32, (SEG, SEG), 1
    )
    scores = (
        jnp.einsum("nqkgd,nskd->nkgqs", query_seg, key_seg, preferred_element_type=jnp.float32)
        * score_scale
    )
    scores = jnp.where(causal, scores, -1e30)
    peak = jnp.max(scores, axis=-1, keepdims=True)
    expd = jnp.exp(scores - peak)
    probs = (expd / jnp.sum(expd, axis=-1, keepdims=True)).astype(jnp.bfloat16)
    local = jnp.einsum("nkgqs,nskd->nqkgd", probs, value_seg, preferred_element_type=jnp.float32)
    gate_mix = jax.nn.sigmoid(gate_bias).reshape(kv_local, group)
    mixed = (
        gate_mix[None, None, :, :, None] * retrieved
        + (1.0 - gate_mix)[None, None, :, :, None] * local
    )
    mixed = mixed.astype(jnp.bfloat16).reshape(token_count, kv_local * group * HD)
    partial_out = jnp.dot(
        mixed, lax.all_gather(wo, "seq", axis=1, tiled=True), preferred_element_type=jnp.float32
    )
    return lax.psum_scatter(
        partial_out.astype(jnp.bfloat16), "head", scatter_dimension=1, tiled=True
    )


def solution(mesh):
    placed = (
        P("seq", None),
        P(),
        P("seq", "head"),
        P("seq", "head"),
        P("seq", "head"),
        P("head", "seq"),
        P("head"),
        P("head", None, None),
        P("head", None),
    )
    return jax.shard_map(
        per_device, mesh=mesh, in_specs=placed, out_specs=P("seq", "head"), check_vma=False
    )
```

profile of v0, /device:TPU:1, one launch (start us, length us, event | category | flops | bytes accessed | tf_op | source)
XLA Modules:
  0.0 559.1 jit_solution(2536971388080526449)
XLA Ops:
  9.5 5.1 fusion.3
  15.2 10.3 %fusion.5 = bf16[1024,4096]{1,0:T(8,128)(2,1)} fusion(bf16[1024,4096]{1,0:T(8,128)(2,1)} %param.11, f32[4096]{0:T(1024)S(1)} %copy-done.2, f32[1024]{0:T(1024)S(1)} %add_rsqrt_fusion), kind=kLoop, calls=%fused_computation.9 | loop fusion | flops 16777216 | bytes 16797696 | tf_op jit(solution)/shard_map/convert_element_type | solution.py:28
  25.5 60.1 %all-gather.5.cloned.1.call-done = bf16[4096,128]{1,0:T(8,128)(2,1)} async-done(((bf16[128,128]{1,0:T(8,128)(2,1)}), bf16[4096,128]{1,0:T(8,128)(2,1)}) %all-gather.5.cloned.1.call-update) | async-done | bytes 1048592 | tf_op jit(solution)/shard_map/all_gather | solution.py:35
  85.6 6.0 %fusion.38 = (f32[128]{0:T(128)S(1)}, bf16[1024,128]{1,0:T(8,128)(2,1)S(1)}) fusion(bf16[1024,4096]{1,0:T(8,128)(2,1)} %fusion.5, bf16[4096,128]{1,0:T(8,128)(2,1)} %all-gather.5.cloned.1.call-done), kind=kOutput, calls=%fused_computation.57 | convolution fusion | flops 1074659200 | bytes 9699840 | tf_op jit(solution)/shard_map/dot_general | solution.py:32
  91.7 70.3 %all-gather.7.cloned.1.call-done = bf16[4096,128]{1,0:T(8,128)(2,1)} async-done(((bf16[128,128]{1,0:T(8,128)(2,1)}), bf16[4096,128]{1,0:T(8,128)(2,1)}) %all-gather.7.cloned.1.call-update) | async-done | bytes 1048592 | tf_op jit(solution)/shard_map/all_gather | solution.py:36
  162.0 5.9 %convolution_convert_fusion.2 = bf16[1024,128]{1,0:T(8,128)(2,1)S(1)} fusion(bf16[1024,4096]{1,0:T(8,128)(2,1)} %fusion.5, bf16[4096,128]{1,0:T(8,128)(2,1)} %all-gather.7.cloned.1.call-done), kind=kOutput, calls=%fused_computation.32 | convolution fusion | flops 1073872896 | bytes 9699328 | tf_op jit(solution)/shard_map/dot_general | solution.py:32
  168.9 253.9 %while.13 = (s32[]{:T(128)}, f32[1,128,128]{2,1,0:T(8,128)S(1)}, f32[1,128]{1,0:T(1,128)S(1)}, f32[1,128,128]{2,1,0:T(8,128)S(1)}, f32[1,128]{1,0:T(1,128)S(1)}, /*index=5*/s32[]{:T(128)}, s32[]{:T(128)}) while((s32[]{:T(128)}, f32[1,128,128]{2,1,0:T(8,128)S(1)}, f32[1,128]{1,0:T(1,128)S(1)}, f32[1,128,128]{2,1,0:T(8,128)S(1)}, ...), condition=%wide.region_4.5_spmd.clone, body=%wide.region_3.4_spmd.clone.sunk | while | flops 66051 | bytes 396456 | solution.py:62
  171.1 4.0 collective-permute-start.1
  182.2 4.0 collective-permute-start
  197.8 4.0 collective-permute-start
  221.2 4.0 collective-permute-start
  229.8 4.0 collective-permute-start
  233.8 4.0 collective-permute-start.1
  238.5 4.0 collective-permute-start
  246.9 4.0 collective-permute-start
  279.8 4.0 collective-permute-start
  292.2 4.0 collective-permute-start.1
  305.1 4.0 collective-permute-start
  313.5 4.0 collective-permute-start
  317.5 4.1 collective-permute-start.1
  322.4 4.0 collective-permute-start
  330.8 4.0 collective-permute-start
  334.8 4.4 collective-permute-start.1
  340.0 4.0 collective-permute-start
  367.7 4.3 collective-permute-start.1
  384.6 4.1 collective-permute-start.1
  401.3 4.0 collective-permute-start.1
  409.7 4.0 collective-permute-start.1
  418.1 4.0 collective-permute-start.1
  422.9 9.0 %convolution_convert_fusion.1 = bf16[1024,512]{1,0:T(8,128)(2,1)S(1)} fusion(bf16[1024,4096]{1,0:T(8,128)(2,1)} %fusion.5, bf16[4096,512]{1,0:T(8,128)(2,1)} %all-gather.9.cloned.1.call-done), kind=kOutput, calls=%fused_computation.31 | convolution fusion | flops 4295491584 | bytes 13631488 | tf_op jit(solution)/shard_map/dot_general | solution.py:32
  445.5 8.9 %convolution_convert_fusion = bf16[1024,4096]{1,0:T(8,128)(2,1)} fusion(bf16[512,4096]{1,0:T(8,128)(2,1)} %all-gather.11.cloned.1.call-done, bf16[128,8,4,128]{3,2,1,0:T(4,128)(2,1)S(1)} %bitcast.93), kind=kOutput, calls=%fused_computation.13 | convolution fusion | flops 4299161600 | bytes 13631488 | tf_op jit(solution)/shard_map/dot_general | solution.py:92
  454.5 98.1 %reduce-scatter.2.cloned.1.call-done = bf16[1024,512]{1,0:T(8,128)(2,1)} async-done(((bf16[1024,4096]{1,0:T(8,128)(2,1)}), bf16[1024,512]{1,0:T(8,128)(2,1)}) %reduce-scatter.2.cloned.1.call-update) | async-done | bytes 1048592 | tf_op jit(solution)/shard_map/reduce_scatter | solution.py:95
  (277 shorter events, 181.8 us)
Async XLA Ops:
  6.5 79.0 %all-gather.5.cloned.1.call-start = ((), (), s32[]{:S(2)}) async-start(), calls=%async_computation.1 | async-start | bytes 1081344 | tf_op jit(solution)/shard_map/all_gather | solution.py:35
  7.3 154.7 %all-gather.7.cloned.1.call-start = ((), (), s32[]{:S(2)}) async-start(), calls=%async_computation.2 | async-start | bytes 1081344 | tf_op jit(solution)/shard_map/all_gather | solution.py:36
  8.0 414.9 %all-gather.9.cloned.1.call-start = ((), (), s32[]{:S(2)}) async-start(), calls=%async_computation.3 | async-start | bytes 4325376 | tf_op jit(solution)/shard_map/all_gather | solution.py:34
  8.7 436.8 %all-gather.11.cloned.1.call-start = ((), (), s32[]{:S(2)}) async-start(), calls=%async_computation.4 | async-start | bytes 4325376 | tf_op jit(solution)/shard_map/all_gather | solution.py:93
  9.3 543.3 %reduce-scatter.2.cloned.1.call-start = ((), (), s32[]{:S(2)}) async-start(), calls=%async_computation.5 | async-start | bytes 9437184 | tf_op jit(solution)/shard_map/reduce_scatter | solution.py:95
  182.2 8.1 %collective-permute-start = (bf16[1,128,128]{2,1,0:T(8,128)(2,1)S(1)}, bf16[1,128,128]{2,1,0:T(8,128)(2,1)S(1)}, u32[]{:S(2)}, u32[]{:S(2)}) collective-permute-start(bf16[1,128,128]{2,1,0:T(8,128)(2,1)S(1)} %fusion.74), channel_id=1, source_target_pairs={{0,8},{8,16},{16,24},{24,32},{32,40},{40,48},{48,56},{56,64},{64,7... | collective-permute-start | bytes 98312 | tf_op jit(solution)/shard_map/while/body/eval_jaxpr/ppermute | solution.py:16
  197.8 8.1 %collective-permute-start = (bf16[1,128,128]{2,1,0:T(8,128)(2,1)S(1)}, bf16[1,128,128]{2,1,0:T(8,128)(2,1)S(1)}, u32[]{:S(2)}, u32[]{:S(2)}) collective-permute-start(bf16[1,128,128]{2,1,0:T(8,128)(2,1)S(1)} %fusion.74), channel_id=1, source_target_pairs={{0,8},{8,16},{16,24},{24,32},{32,40},{40,48},{48,56},{56,64},{64,7... | collective-permute-start | bytes 98312 | tf_op jit(solution)/shard_map/while/body/eval_jaxpr/ppermute | solution.py:16
  205.9 7.8 %collective-permute-start = (bf16[1,128,128]{2,1,0:T(8,128)(2,1)S(1)}, bf16[1,128,128]{2,1,0:T(8,128)(2,1)S(1)}, u32[]{:S(2)}, u32[]{:S(2)}) collective-permute-start(bf16[1,128,128]{2,1,0:T(8,128)(2,1)S(1)} %fusion.74), channel_id=1, source_target_pairs={{0,8},{8,16},{16,24},{24,32},{32,40},{40,48},{48,56},{56,64},{64,7... | collective-permute-start | bytes 98312 | tf_op jit(solution)/shard_map/while/body/eval_jaxpr/ppermute | solution.py:16
  221.2 8.5 %collective-permute-start = (bf16[1,128,128]{2,1,0:T(8,128)(2,1)S(1)}, bf16[1,128,128]{2,1,0:T(8,128)(2,1)S(1)}, u32[]{:S(2)}, u32[]{:S(2)}) collective-permute-start(bf16[1,128,128]{2,1,0:T(8,128)(2,1)S(1)} %fusion.74), channel_id=1, source_target_pairs={{0,8},{8,16},{16,24},{24,32},{32,40},{40,48},{48,56},{56,64},{64,7... | collective-permute-start | bytes 98312 | tf_op jit(solution)/shard_map/while/body/eval_jaxpr/ppermute | solution.py:16
  229.8 8.7 %collective-permute-start = (bf16[1,128,128]{2,1,0:T(8,128)(2,1)S(1)}, bf16[1,128,128]{2,1,0:T(8,128)(2,1)S(1)}, u32[]{:S(2)}, u32[]{:S(2)}) collective-permute-start(bf16[1,128,128]{2,1,0:T(8,128)(2,1)S(1)} %fusion.74), channel_id=1, source_target_pairs={{0,8},{8,16},{16,24},{24,32},{32,40},{40,48},{48,56},{56,64},{64,7... | collective-permute-start | bytes 98312 | tf_op jit(solution)/shard_map/while/body/eval_jaxpr/ppermute | solution.py:16
  238.5 8.3 %collective-permute-start = (bf16[1,128,128]{2,1,0:T(8,128)(2,1)S(1)}, bf16[1,128,128]{2,1,0:T(8,128)(2,1)S(1)}, u32[]{:S(2)}, u32[]{:S(2)}) collective-permute-start(bf16[1,128,128]{2,1,0:T(8,128)(2,1)S(1)} %fusion.74), channel_id=1, source_target_pairs={{0,8},{8,16},{16,24},{24,32},{32,40},{40,48},{48,56},{56,64},{64,7... | collective-permute-start | bytes 98312 | tf_op jit(solution)/shard_map/while/body/eval_jaxpr/ppermute | solution.py:16
  246.9 8.3 %collective-permute-start = (bf16[1,128,128]{2,1,0:T(8,128)(2,1)S(1)}, bf16[1,128,128]{2,1,0:T(8,128)(2,1)S(1)}, u32[]{:S(2)}, u32[]{:S(2)}) collective-permute-start(bf16[1,128,128]{2,1,0:T(8,128)(2,1)S(1)} %fusion.74), channel_id=1, source_target_pairs={{0,8},{8,16},{16,24},{24,32},{32,40},{40,48},{48,56},{56,64},{64,7... | collective-permute-start | bytes 98312 | tf_op jit(solution)/shard_map/while/body/eval_jaxpr/ppermute | solution.py:16
  255.2 8.3 %collective-permute-start = (bf16[1,128,128]{2,1,0:T(8,128)(2,1)S(1)}, bf16[1,128,128]{2,1,0:T(8,128)(2,1)S(1)}, u32[]{:S(2)}, u32[]{:S(2)}) collective-permute-start(bf16[1,128,128]{2,1,0:T(8,128)(2,1)S(1)} %fusion.74), channel_id=1, source_target_pairs={{0,8},{8,16},{16,24},{24,32},{32,40},{40,48},{48,56},{56,64},{64,7... | collective-permute-start | bytes 98312 | tf_op jit(solution)/shard_map/while/body/eval_jaxpr/ppermute | solution.py:16
  263.6 8.3 %collective-permute-start = (bf16[1,128,128]{2,1,0:T(8,128)(2,1)S(1)}, bf16[1,128,128]{2,1,0:T(8,128)(2,1)S(1)}, u32[]{:S(2)}, u32[]{:S(2)}) collective-permute-start(bf16[1,128,128]{2,1,0:T(8,128)(2,1)S(1)} %fusion.74), channel_id=1, source_target_pairs={{0,8},{8,16},{16,24},{24,32},{32,40},{40,48},{48,56},{56,64},{64,7... | collective-permute-start | bytes 98312 | tf_op jit(solution)/shard_map/while/body/eval_jaxpr/ppermute | solution.py:16
  271.9 7.8 %collective-permute-start = (bf16[1,128,128]{2,1,0:T(8,128)(2,1)S(1)}, bf16[1,128,128]{2,1,0:T(8,128)(2,1)S(1)}, u32[]{:S(2)}, u32[]{:S(2)}) collective-permute-start(bf16[1,128,128]{2,1,0:T(8,128)(2,1)S(1)} %fusion.74), channel_id=1, source_target_pairs={{0,8},{8,16},{16,24},{24,32},{32,40},{40,48},{48,56},{56,64},{64,7... | collective-permute-start | bytes 98312 | tf_op jit(solution)/shard_map/while/body/eval_jaxpr/ppermute | solution.py:16
  279.8 8.6 %collective-permute-start = (bf16[1,128,128]{2,1,0:T(8,128)(2,1)S(1)}, bf16[1,128,128]{2,1,0:T(8,128)(2,1)S(1)}, u32[]{:S(2)}, u32[]{:S(2)}) collective-permute-start(bf16[1,128,128]{2,1,0:T(8,128)(2,1)S(1)} %fusion.74), channel_id=1, source_target_pairs={{0,8},{8,16},{16,24},{24,32},{32,40},{40,48},{48,56},{56,64},{64,7... | collective-permute-start | bytes 98312 | tf_op jit(solution)/shard_map/while/body/eval_jaxpr/ppermute | solution.py:16
  288.5 8.5 %collective-permute-start = (bf16[1,128,128]{2,1,0:T(8,128)(2,1)S(1)}, bf16[1,128,128]{2,1,0:T(8,128)(2,1)S(1)}, u32[]{:S(2)}, u32[]{:S(2)}) collective-permute-start(bf16[1,128,128]{2,1,0:T(8,128)(2,1)S(1)} %fusion.74), channel_id=1, source_target_pairs={{0,8},{8,16},{16,24},{24,32},{32,40},{40,48},{48,56},{56,64},{64,7... | collective-permute-start | bytes 98312 | tf_op jit(solution)/shard_map/while/body/eval_jaxpr/ppermute | solution.py:16
  297.0 8.0 %collective-permute-start = (bf16[1,128,128]{2,1,0:T(8,128)(2,1)S(1)}, bf16[1,128,128]{2,1,0:T(8,128)(2,1)S(1)}, u32[]{:S(2)}, u32[]{:S(2)}) collective-permute-start(bf16[1,128,128]{2,1,0:T(8,128)(2,1)S(1)} %fusion.74), channel_id=1, source_target_pairs={{0,8},{8,16},{16,24},{24,32},{32,40},{40,48},{48,56},{56,64},{64,7... | collective-permute-start | bytes 98312 | tf_op jit(solution)/shard_map/while/body/eval_jaxpr/ppermute | solution.py:16
  305.1 8.4 %collective-permute-start = (bf16[1,128,128]{2,1,0:T(8,128)(2,1)S(1)}, bf16[1,128,128]{2,1,0:T(8,128)(2,1)S(1)}, u32[]{:S(2)}, u32[]{:S(2)}) collective-permute-start(bf16[1,128,128]{2,1,0:T(8,128)(2,1)S(1)} %fusion.74), channel_id=1, source_target_pairs={{0,8},{8,16},{16,24},{24,32},{32,40},{40,48},{48,56},{56,64},{64,7... | collective-permute-start | bytes 98312 | tf_op jit(solution)/shard_map/while/body/eval_jaxpr/ppermute | solution.py:16
  313.5 8.8 %collective-permute-start = (bf16[1,128,128]{2,1,0:T(8,128)(2,1)S(1)}, bf16[1,128,128]{2,1,0:T(8,128)(2,1)S(1)}, u32[]{:S(2)}, u32[]{:S(2)}) collective-permute-start(bf16[1,128,128]{2,1,0:T(8,128)(2,1)S(1)} %fusion.74), channel_id=1, source_target_pairs={{0,8},{8,16},{16,24},{24,32},{32,40},{40,48},{48,56},{56,64},{64,7... | collective-permute-start | bytes 98312 | tf_op jit(solution)/shard_map/while/body/eval_jaxpr/ppermute | solution.py:16
  322.4 8.4 %collective-permute-start = (bf16[1,128,128]{2,1,0:T(8,128)(2,1)S(1)}, bf16[1,128,128]{2,1,0:T(8,128)(2,1)S(1)}, u32[]{:S(2)}, u32[]{:S(2)}) collective-permute-start(bf16[1,128,128]{2,1,0:T(8,128)(2,1)S(1)} %fusion.74), channel_id=1, source_target_pairs={{0,8},{8,16},{16,24},{24,32},{32,40},{40,48},{48,56},{56,64},{64,7... | collective-permute-start | bytes 98312 | tf_op jit(solution)/shard_map/while/body/eval_jaxpr/ppermute | solution.py:16
  330.8 9.1 %collective-permute-start = (bf16[1,128,128]{2,1,0:T(8,128)(2,1)S(1)}, bf16[1,128,128]{2,1,0:T(8,128)(2,1)S(1)}, u32[]{:S(2)}, u32[]{:S(2)}) collective-permute-start(bf16[1,128,128]{2,1,0:T(8,128)(2,1)S(1)} %fusion.74), channel_id=1, source_target_pairs={{0,8},{8,16},{16,24},{24,32},{32,40},{40,48},{48,56},{56,64},{64,7... | collective-permute-start | bytes 98312 | tf_op jit(solution)/shard_map/while/body/eval_jaxpr/ppermute | solution.py:16
  340.0 8.3 %collective-permute-start = (bf16[1,128,128]{2,1,0:T(8,128)(2,1)S(1)}, bf16[1,128,128]{2,1,0:T(8,128)(2,1)S(1)}, u32[]{:S(2)}, u32[]{:S(2)}) collective-permute-start(bf16[1,128,128]{2,1,0:T(8,128)(2,1)S(1)} %fusion.74), channel_id=1, source_target_pairs={{0,8},{8,16},{16,24},{24,32},{32,40},{40,48},{48,56},{56,64},{64,7... | collective-permute-start | bytes 98312 | tf_op jit(solution)/shard_map/while/body/eval_jaxpr/ppermute | solution.py:16
  348.3 7.7 %collective-permute-start = (bf16[1,128,128]{2,1,0:T(8,128)(2,1)S(1)}, bf16[1,128,128]{2,1,0:T(8,128)(2,1)S(1)}, u32[]{:S(2)}, u32[]{:S(2)}) collective-permute-start(bf16[1,128,128]{2,1,0:T(8,128)(2,1)S(1)} %fusion.74), channel_id=1, source_target_pairs={{0,8},{8,16},{16,24},{24,32},{32,40},{40,48},{48,56},{56,64},{64,7... | collective-permute-start | bytes 98312 | tf_op jit(solution)/shard_map/while/body/eval_jaxpr/ppermute | solution.py:16
  356.1 8.0 %collective-permute-start = (bf16[1,128,128]{2,1,0:T(8,128)(2,1)S(1)}, bf16[1,128,128]{2,1,0:T(8,128)(2,1)S(1)}, u32[]{:S(2)}, u32[]{:S(2)}) collective-permute-start(bf16[1,128,128]{2,1,0:T(8,128)(2,1)S(1)} %fusion.74), channel_id=1, source_target_pairs={{0,8},{8,16},{16,24},{24,32},{32,40},{40,48},{48,56},{56,64},{64,7... | collective-permute-start | bytes 98312 | tf_op jit(solution)/shard_map/while/body/eval_jaxpr/ppermute | solution.py:16
  364.1 8.6 %collective-permute-start = (bf16[1,128,128]{2,1,0:T(8,128)(2,1)S(1)}, bf16[1,128,128]{2,1,0:T(8,128)(2,1)S(1)}, u32[]{:S(2)}, u32[]{:S(2)}) collective-permute-start(bf16[1,128,128]{2,1,0:T(8,128)(2,1)S(1)} %fusion.74), channel_id=1, source_target_pairs={{0,8},{8,16},{16,24},{24,32},{32,40},{40,48},{48,56},{56,64},{64,7... | collective-permute-start | bytes 98312 | tf_op jit(solution)/shard_map/while/body/eval_jaxpr/ppermute | solution.py:16
  372.8 8.2 %collective-permute-start = (bf16[1,128,128]{2,1,0:T(8,128)(2,1)S(1)}, bf16[1,128,128]{2,1,0:T(8,128)(2,1)S(1)}, u32[]{:S(2)}, u32[]{:S(2)}) collective-permute-start(bf16[1,128,128]{2,1,0:T(8,128)(2,1)S(1)} %fusion.74), channel_id=1, source_target_pairs={{0,8},{8,16},{16,24},{24,32},{32,40},{40,48},{48,56},{56,64},{64,7... | collective-permute-start | bytes 98312 | tf_op jit(solution)/shard_map/while/body/eval_jaxpr/ppermute | solution.py:16
  381.0 8.4 %collective-permute-start = (bf16[1,128,128]{2,1,0:T(8,128)(2,1)S(1)}, bf16[1,128,128]{2,1,0:T(8,128)(2,1)S(1)}, u32[]{:S(2)}, u32[]{:S(2)}) collective-permute-start(bf16[1,128,128]{2,1,0:T(8,128)(2,1)S(1)} %fusion.74), channel_id=1, source_target_pairs={{0,8},{8,16},{16,24},{24,32},{32,40},{40,48},{48,56},{56,64},{64,7... | collective-permute-start | bytes 98312 | tf_op jit(solution)/shard_map/while/body/eval_jaxpr/ppermute | solution.py:16
  389.5 8.2 %collective-permute-start = (bf16[1,128,128]{2,1,0:T(8,128)(2,1)S(1)}, bf16[1,128,128]{2,1,0:T(8,128)(2,1)S(1)}, u32[]{:S(2)}, u32[]{:S(2)}) collective-permute-start(bf16[1,128,128]{2,1,0:T(8,128)(2,1)S(1)} %fusion.74), channel_id=1, source_target_pairs={{0,8},{8,16},{16,24},{24,32},{32,40},{40,48},{48,56},{56,64},{64,7... | collective-permute-start | bytes 98312 | tf_op jit(solution)/shard_map/while/body/eval_jaxpr/ppermute | solution.py:16
  397.8 8.3 %collective-permute-start = (bf16[1,128,128]{2,1,0:T(8,128)(2,1)S(1)}, bf16[1,128,128]{2,1,0:T(8,128)(2,1)S(1)}, u32[]{:S(2)}, u32[]{:S(2)}) collective-permute-start(bf16[1,128,128]{2,1,0:T(8,128)(2,1)S(1)} %fusion.74), channel_id=1, source_target_pairs={{0,8},{8,16},{16,24},{24,32},{32,40},{40,48},{48,56},{56,64},{64,7... | collective-permute-start | bytes 98312 | tf_op jit(solution)/shard_map/while/body/eval_jaxpr/ppermute | solution.py:16
  406.1 8.3 %collective-permute-start = (bf16[1,128,128]{2,1,0:T(8,128)(2,1)S(1)}, bf16[1,128,128]{2,1,0:T(8,128)(2,1)S(1)}, u32[]{:S(2)}, u32[]{:S(2)}) collective-permute-start(bf16[1,128,128]{2,1,0:T(8,128)(2,1)S(1)} %fusion.74), channel_id=1, source_target_pairs={{0,8},{8,16},{16,24},{24,32},{32,40},{40,48},{48,56},{56,64},{64,7... | collective-permute-start | bytes 98312 | tf_op jit(solution)/shard_map/while/body/eval_jaxpr/ppermute | solution.py:16
  414.5 8.3 %collective-permute-start = (bf16[1,128,128]{2,1,0:T(8,128)(2,1)S(1)}, bf16[1,128,128]{2,1,0:T(8,128)(2,1)S(1)}, u32[]{:S(2)}, u32[]{:S(2)}) collective-permute-start(bf16[1,128,128]{2,1,0:T(8,128)(2,1)S(1)} %fusion.74), channel_id=1, source_target_pairs={{0,8},{8,16},{16,24},{24,32},{32,40},{40,48},{48,56},{56,64},{64,7... | collective-permute-start | bytes 98312 | tf_op jit(solution)/shard_map/while/body/eval_jaxpr/ppermute | solution.py:16
  (44 other events, 1188.7 us)
Sparse Core Ops, SparseCore 0:
  10.0 75.5 all-gather.4
  88.2 73.7 all-gather.6
  164.6 81.8 all-gather.8
  248.8 82.8 all-gather.10
  454.6 97.9 reduce-scatter.1
where the time goes:
time: 565 us; the launch traced here: 559 us
  waiting for transfers between devices  253 us (45%)
  starting transfers between devices  230 us (41%)
  matrix products  40.5 us (7%)
  other arithmetic  19.2 us (3%)
  between operations  13.4 us (2%)
    ppermute x62, starting transfers between devices, from_behind(): return lax.ppermute(block, axis, route)  230 us
    reduce_scatter x1, waiting for transfers between devices, per_device(): lax.psum_scatter(partial_out.astype(jnp.bfloat16), 'head', scatter_dimens...  98.1 us
    all_gather x1, waiting for transfers between devices, per_device(): value_wide = project(lax.all_gather(wv, 'seq', axis=0, tiled=True))  70.3 us
    all_gather x1, waiting for transfers between devices, per_device(): key_wide = project(lax.all_gather(wk, 'seq', axis=0, tiled=True))  60.1 us
    ppermute x62, waiting for transfers between devices, from_behind(): return lax.ppermute(block, axis, route)  21.9 us
    dot_general x3, matrix products, project(): return jnp.dot(normed, shard_piece, preferred_element_type=jnp.float32)  20.9 us
  transfers between devices with their start and end apart: 67, of which 34 were waited for; matrix products, arithmetic and copies ran while one was open for 9% of the time, Pallas kernels for 0%

commit v1 on v0

--- a/solution.py
+++ b/solution.py
@@ -32,7 +32,14 @@
         return jnp.dot(normed, shard_piece, preferred_element_type=jnp.float32)
 
     query_wide = project(lax.all_gather(wq, "seq", axis=0, tiled=True))
-    key_wide = project(lax.all_gather(wk, "seq", axis=0, tiled=True))
+    key_wide = project(
+        jnp.concatenate(
+            lax.all_to_all(
+                jnp.stack([wk] * lax.axis_size("seq")), split_axis=0, concat_axis=0, axis_name="seq"
+            ),
+            axis=0,
+        )
+    )
     value_wide = project(lax.all_gather(wv, "seq", axis=0, tiled=True))
     queries = query_wide.astype(jnp.bfloat16)
     keys_all = key_wide.astype(jnp.bfloat16)

time: 565 us -> 490 us (0.87)
  waiting for transfers between devices: 253 us -> 164 us
  starting transfers between devices: 230 us -> 242 us
    all_gather x1 -> x0, waiting for transfers between devices: 60.1 us -> none  [per_device(): key_wide = project(lax.all_gather(wk, 'seq', axis=0, tiled=True))]
    all_gather x1, waiting for transfers between devices: 70.3 us -> 33.1 us  [per_device(): value_wide = project(lax.all_gather(wv, 'seq', axis=0, tiled=True))]
    all_to_all x0 -> x1, starting transfers between devices: none -> 12 us  [per_device(): lax.all_to_all(jnp.stack([wk] * lax.axis_size('seq')), split_axis=0, conc...]
    all_to_all x0 -> x1, waiting for transfers between devices: none -> 8.47 us  [per_device(): lax.all_to_all(jnp.stack([wk] * lax.axis_size('seq')), split_axis=0, conc...]
  transfers between devices with their start and end apart: 67 -> 67, of which waited for: 34 -> 34; matrix products, arithmetic and copies ran while one was open for 9% -> 11% of each run, Pallas kernels for 0% -> 0%
where the time goes in v1:
time: 490 us; the launch traced here: 484 us
  starting transfers between devices  242 us (49%)
  waiting for transfers between devices  164 us (33%)
  matrix products  40.3 us (8%)
  other arithmetic  19.9 us (4%)
  between operations  13.4 us (3%)
    ppermute x62, starting transfers between devices, from_behind(): return lax.ppermute(block, axis, route)  230 us
    reduce_scatter x1, waiting for transfers between devices, per_device(): lax.psum_scatter(partial_out.astype(jnp.bfloat16), 'head', scatter_dimens...  98.1 us
    all_gather x1, waiting for transfers between devices, per_device(): value_wide = project(lax.all_gather(wv, 'seq', axis=0, tiled=True))  33.1 us
    ppermute x62, waiting for transfers between devices, from_behind(): return lax.ppermute(block, axis, route)  21.9 us
    dot_general x3, matrix products, project(): return jnp.dot(normed, shard_piece, preferred_element_type=jnp.float32)  20.7 us
    all_to_all x1, starting transfers between devices, per_device(): lax.all_to_all(jnp.stack([wk] * lax.axis_size('seq')), split_axis=0, conc...  12 us
    convert_element_type x1, other arithmetic, per_device(): normed = (widened * lax.rsqrt(jnp.mean(widened * widened, axis=-1, keepdi...  10.3 us
  transfers between devices with their start and end apart: 67, of which 34 were waited for; matrix products, arithmetic and copies ran while one was open for 11% of the time, Pallas kernels for 0%

profile of v1, /device:TPU:1, one launch (start us, length us, event | category | flops | bytes accessed | tf_op | source)
XLA Modules:
  0.0 484.2 jit_solution(9521950406188183402)
XLA Ops:
  10.0 12.0 %all-to-all-start = ((bf16[32,128,128]{2,1,0:T(8,128)(2,1)}), bf16[32,128,128]{2,1,0:T(8,128)(2,1)S(1)}, u32[]{:S(2)}, u32[]{:S(2)}) async-start(bf16[32,128,128]{2,1,0:T(8,128)(2,1)} %stack.2), calls=%async_computation | async-start | bytes 2097152 | tf_op jit(solution)/shard_map/all_to_all | solution.py:37
  24.2 5.1 %fusion.3 = f32[1024]{0:T(1024)S(1)} fusion(bf16[1024,4096]{1,0:T(8,128)(2,1)} %param.11), kind=kLoop, calls=%fused_computation.7 | loop fusion | flops 12581888 | bytes 8392704 | tf_op jit(solution)/shard_map/reduce_sum | solution.py:27
  29.3 10.3 %fusion.5 = bf16[1024,4096]{1,0:T(8,128)(2,1)} fusion(bf16[1024,4096]{1,0:T(8,128)(2,1)} %param.11, f32[4096]{0:T(1024)S(1)} %copy-done.2, f32[1024]{0:T(1024)S(1)} %add_rsqrt_fusion), kind=kLoop, calls=%fused_computation.9 | loop fusion | flops 16777216 | bytes 16797696 | tf_op jit(solution)/shard_map/convert_element_type | solution.py:28
  39.6 8.5 %all-to-all-done = bf16[32,128,128]{2,1,0:T(8,128)(2,1)S(1)} async-done(((bf16[32,128,128]{2,1,0:T(8,128)(2,1)}), bf16[32,128,128]{2,1,0:T(8,128)(2,1)S(1)}, u32[]{:S(2)}, u32[]{:S(2)}) %all-to-all-start) | async-done | bytes 1048608 | tf_op jit(solution)/shard_map/all_to_all | solution.py:37
  48.1 5.7 %fusion.38 = (f32[128]{0:T(128)S(1)}, bf16[1024,128]{1,0:T(8,128)(2,1)S(1)}) fusion(bf16[1024,4096]{1,0:T(8,128)(2,1)} %fusion.5, bf16[4096,128]{1,0:T(8,128)(2,1)S(1)} %bitcast.94), kind=kOutput, calls=%fused_computation.57 | convolution fusion | flops 1074659200 | bytes 9699840 | tf_op jit(solution)/shard_map/dot_general | solution.py:32
  54.0 33.1 %all-gather.4.cloned.1.call-done = bf16[4096,128]{1,0:T(8,128)(2,1)} async-done(((bf16[128,128]{1,0:T(8,128)(2,1)}), bf16[4096,128]{1,0:T(8,128)(2,1)}) %all-gather.4.cloned.1.call-update) | async-done | bytes 1048592 | tf_op jit(solution)/shard_map/all_gather | solution.py:43
  87.1 5.9 %convolution_convert_fusion.2 = bf16[1024,128]{1,0:T(8,128)(2,1)S(1)} fusion(bf16[1024,4096]{1,0:T(8,128)(2,1)} %fusion.5, bf16[4096,128]{1,0:T(8,128)(2,1)} %all-gather.4.cloned.1.call-done), kind=kOutput, calls=%fused_computation.32 | convolution fusion | flops 1073872896 | bytes 9699328 | tf_op jit(solution)/shard_map/dot_general | solution.py:32
  94.0 254.0 %while.13 = (s32[]{:T(128)}, f32[1,128,128]{2,1,0:T(8,128)S(1)}, f32[1,128]{1,0:T(1,128)S(1)}, f32[1,128,128]{2,1,0:T(8,128)S(1)}, f32[1,128]{1,0:T(1,128)S(1)}, /*index=5*/s32[]{:T(128)}, s32[]{:T(128)}) while((s32[]{:T(128)}, f32[1,128,128]{2,1,0:T(8,128)S(1)}, f32[1,128]{1,0:T(1,128)S(1)}, f32[1,128,128]{2,1,0:T(8,128)S(1)}, ...), condition=%wide.region_4.5_spmd.clone, body=%wide.region_3.4_spmd.clone.sunk | while | flops 66051 | bytes 396456 | solution.py:69
  96.3 4.0 collective-permute-start.1
  107.3 4.0 collective-permute-start
  122.9 4.0 collective-permute-start
  146.4 4.0 collective-permute-start
  154.9 4.0 collective-permute-start
  158.9 4.0 collective-permute-start.1
  163.7 4.0 collective-permute-start
  172.0 4.0 collective-permute-start
  208.9 4.0 collective-permute-start.1
  225.6 4.0 collective-permute-start.1
  230.4 4.0 collective-permute-start
  234.4 4.1 collective-permute-start.1
  239.2 4.0 collective-permute-start
  243.2 4.0 collective-permute-start.1
  248.0 4.0 collective-permute-start
  259.6 4.8 collective-permute-start.1
  292.9 4.3 collective-permute-start.1
  309.8 4.1 collective-permute-start.1
  326.5 4.0 collective-permute-start.1
  334.8 4.0 collective-permute-start.1
  343.2 4.0 collective-permute-start.1
  348.1 9.1 %convolution_convert_fusion.1 = bf16[1024,512]{1,0:T(8,128)(2,1)S(1)} fusion(bf16[1024,4096]{1,0:T(8,128)(2,1)} %fusion.5, bf16[4096,512]{1,0:T(8,128)(2,1)} %all-gather.6.cloned.1.call-done), kind=kOutput, calls=%fused_computation.31 | convolution fusion | flops 4295491584 | bytes 13631488 | tf_op jit(solution)/shard_map/dot_general | solution.py:32
  370.7 8.9 %convolution_convert_fusion = bf16[1024,4096]{1,0:T(8,128)(2,1)} fusion(bf16[512,4096]{1,0:T(8,128)(2,1)} %all-gather.8.cloned.1.call-done, bf16[128,8,4,128]{3,2,1,0:T(4,128)(2,1)S(1)} %bitcast.95), kind=kOutput, calls=%fused_computation.13 | convolution fusion | flops 4299161600 | bytes 13631488 | tf_op jit(solution)/shard_map/dot_general | solution.py:99
  379.6 98.1 %reduce-scatter.2.cloned.1.call-done = bf16[1024,512]{1,0:T(8,128)(2,1)} async-done(((bf16[1024,4096]{1,0:T(8,128)(2,1)}), bf16[1024,512]{1,0:T(8,128)(2,1)}) %reduce-scatter.2.cloned.1.call-update) | async-done | bytes 1048592 | tf_op jit(solution)/shard_map/reduce_scatter | solution.py:102
  (275 shorter events, 187.5 us)
Async XLA Ops:
  6.5 80.6 %all-gather.4.cloned.1.call-start = ((), (), s32[]{:S(2)}) async-start(), calls=%async_computation.2 | async-start | bytes 1081344 | tf_op jit(solution)/shard_map/all_gather | solution.py:43
  7.3 340.8 %all-gather.6.cloned.1.call-start = ((), (), s32[]{:S(2)}) async-start(), calls=%async_computation.3 | async-start | bytes 4325376 | tf_op jit(solution)/shard_map/all_gather | solution.py:34
  10.0 38.1 %all-to-all-start = ((bf16[32,128,128]{2,1,0:T(8,128)(2,1)}), bf16[32,128,128]{2,1,0:T(8,128)(2,1)S(1)}, u32[]{:S(2)}, u32[]{:S(2)}) async-start(bf16[32,128,128]{2,1,0:T(8,128)(2,1)} %stack.2), calls=%async_computation | async-start | bytes 2097152 | tf_op jit(solution)/shard_map/all_to_all | solution.py:37
  22.0 348.7 %all-gather.8.cloned.1.call-start = ((), (), s32[]{:S(2)}) async-start(), calls=%async_computation.4 | async-start | bytes 4325376 | tf_op jit(solution)/shard_map/all_gather | solution.py:100
  22.8 455.0 %reduce-scatter.2.cloned.1.call-start = ((), (), s32[]{:S(2)}) async-start(), calls=%async_computation.5 | async-start | bytes 9437184 | tf_op jit(solution)/shard_map/reduce_scatter | solution.py:102
  107.3 8.1 %collective-permute-start = (bf16[1,128,128]{2,1,0:T(8,128)(2,1)S(1)}, bf16[1,128,128]{2,1,0:T(8,128)(2,1)S(1)}, u32[]{:S(2)}, u32[]{:S(2)}) collective-permute-start(bf16[1,128,128]{2,1,0:T(8,128)(2,1)S(1)} %fusion.74), channel_id=1, source_target_pairs={{0,8},{8,16},{16,24},{24,32},{32,40},{40,48},{48,56},{56,64},{64,7... | collective-permute-start | bytes 98312 | tf_op jit(solution)/shard_map/while/body/eval_jaxpr/ppermute | solution.py:16
  122.9 8.1 %collective-permute-start = (bf16[1,128,128]{2,1,0:T(8,128)(2,1)S(1)}, bf16[1,128,128]{2,1,0:T(8,128)(2,1)S(1)}, u32[]{:S(2)}, u32[]{:S(2)}) collective-permute-start(bf16[1,128,128]{2,1,0:T(8,128)(2,1)S(1)} %fusion.74), channel_id=1, source_target_pairs={{0,8},{8,16},{16,24},{24,32},{32,40},{40,48},{48,56},{56,64},{64,7... | collective-permute-start | bytes 98312 | tf_op jit(solution)/shard_map/while/body/eval_jaxpr/ppermute | solution.py:16
  131.0 7.8 %collective-permute-start = (bf16[1,128,128]{2,1,0:T(8,128)(2,1)S(1)}, bf16[1,128,128]{2,1,0:T(8,128)(2,1)S(1)}, u32[]{:S(2)}, u32[]{:S(2)}) collective-permute-start(bf16[1,128,128]{2,1,0:T(8,128)(2,1)S(1)} %fusion.74), channel_id=1, source_target_pairs={{0,8},{8,16},{16,24},{24,32},{32,40},{40,48},{48,56},{56,64},{64,7... | collective-permute-start | bytes 98312 | tf_op jit(solution)/shard_map/while/body/eval_jaxpr/ppermute | solution.py:16
  146.4 8.5 %collective-permute-start = (bf16[1,128,128]{2,1,0:T(8,128)(2,1)S(1)}, bf16[1,128,128]{2,1,0:T(8,128)(2,1)S(1)}, u32[]{:S(2)}, u32[]{:S(2)}) collective-permute-start(bf16[1,128,128]{2,1,0:T(8,128)(2,1)S(1)} %fusion.74), channel_id=1, source_target_pairs={{0,8},{8,16},{16,24},{24,32},{32,40},{40,48},{48,56},{56,64},{64,7... | collective-permute-start | bytes 98312 | tf_op jit(solution)/shard_map/while/body/eval_jaxpr/ppermute | solution.py:16
  154.9 8.7 %collective-permute-start = (bf16[1,128,128]{2,1,0:T(8,128)(2,1)S(1)}, bf16[1,128,128]{2,1,0:T(8,128)(2,1)S(1)}, u32[]{:S(2)}, u32[]{:S(2)}) collective-permute-start(bf16[1,128,128]{2,1,0:T(8,128)(2,1)S(1)} %fusion.74), channel_id=1, source_target_pairs={{0,8},{8,16},{16,24},{24,32},{32,40},{40,48},{48,56},{56,64},{64,7... | collective-permute-start | bytes 98312 | tf_op jit(solution)/shard_map/while/body/eval_jaxpr/ppermute | solution.py:16
  163.7 8.3 %collective-permute-start = (bf16[1,128,128]{2,1,0:T(8,128)(2,1)S(1)}, bf16[1,128,128]{2,1,0:T(8,128)(2,1)S(1)}, u32[]{:S(2)}, u32[]{:S(2)}) collective-permute-start(bf16[1,128,128]{2,1,0:T(8,128)(2,1)S(1)} %fusion.74), channel_id=1, source_target_pairs={{0,8},{8,16},{16,24},{24,32},{32,40},{40,48},{48,56},{56,64},{64,7... | collective-permute-start | bytes 98312 | tf_op jit(solution)/shard_map/while/body/eval_jaxpr/ppermute | solution.py:16
  172.0 8.3 %collective-permute-start = (bf16[1,128,128]{2,1,0:T(8,128)(2,1)S(1)}, bf16[1,128,128]{2,1,0:T(8,128)(2,1)S(1)}, u32[]{:S(2)}, u32[]{:S(2)}) collective-permute-start(bf16[1,128,128]{2,1,0:T(8,128)(2,1)S(1)} %fusion.74), channel_id=1, source_target_pairs={{0,8},{8,16},{16,24},{24,32},{32,40},{40,48},{48,56},{56,64},{64,7... | collective-permute-start | bytes 98312 | tf_op jit(solution)/shard_map/while/body/eval_jaxpr/ppermute | solution.py:16
  180.3 8.4 %collective-permute-start = (bf16[1,128,128]{2,1,0:T(8,128)(2,1)S(1)}, bf16[1,128,128]{2,1,0:T(8,128)(2,1)S(1)}, u32[]{:S(2)}, u32[]{:S(2)}) collective-permute-start(bf16[1,128,128]{2,1,0:T(8,128)(2,1)S(1)} %fusion.74), channel_id=1, source_target_pairs={{0,8},{8,16},{16,24},{24,32},{32,40},{40,48},{48,56},{56,64},{64,7... | collective-permute-start | bytes 98312 | tf_op jit(solution)/shard_map/while/body/eval_jaxpr/ppermute | solution.py:16
  188.7 8.3 %collective-permute-start = (bf16[1,128,128]{2,1,0:T(8,128)(2,1)S(1)}, bf16[1,128,128]{2,1,0:T(8,128)(2,1)S(1)}, u32[]{:S(2)}, u32[]{:S(2)}) collective-permute-start(bf16[1,128,128]{2,1,0:T(8,128)(2,1)S(1)} %fusion.74), channel_id=1, source_target_pairs={{0,8},{8,16},{16,24},{24,32},{32,40},{40,48},{48,56},{56,64},{64,7... | collective-permute-start | bytes 98312 | tf_op jit(solution)/shard_map/while/body/eval_jaxpr/ppermute | solution.py:16
  197.1 7.9 %collective-permute-start = (bf16[1,128,128]{2,1,0:T(8,128)(2,1)S(1)}, bf16[1,128,128]{2,1,0:T(8,128)(2,1)S(1)}, u32[]{:S(2)}, u32[]{:S(2)}) collective-permute-start(bf16[1,128,128]{2,1,0:T(8,128)(2,1)S(1)} %fusion.74), channel_id=1, source_target_pairs={{0,8},{8,16},{16,24},{24,32},{32,40},{40,48},{48,56},{56,64},{64,7... | collective-permute-start | bytes 98312 | tf_op jit(solution)/shard_map/while/body/eval_jaxpr/ppermute | solution.py:16
  205.0 8.6 %collective-permute-start = (bf16[1,128,128]{2,1,0:T(8,128)(2,1)S(1)}, bf16[1,128,128]{2,1,0:T(8,128)(2,1)S(1)}, u32[]{:S(2)}, u32[]{:S(2)}) collective-permute-start(bf16[1,128,128]{2,1,0:T(8,128)(2,1)S(1)} %fusion.74), channel_id=1, source_target_pairs={{0,8},{8,16},{16,24},{24,32},{32,40},{40,48},{48,56},{56,64},{64,7... | collective-permute-start | bytes 98312 | tf_op jit(solution)/shard_map/while/body/eval_jaxpr/ppermute | solution.py:16
  213.6 8.3 %collective-permute-start = (bf16[1,128,128]{2,1,0:T(8,128)(2,1)S(1)}, bf16[1,128,128]{2,1,0:T(8,128)(2,1)S(1)}, u32[]{:S(2)}, u32[]{:S(2)}) collective-permute-start(bf16[1,128,128]{2,1,0:T(8,128)(2,1)S(1)} %fusion.74), channel_id=1, source_target_pairs={{0,8},{8,16},{16,24},{24,32},{32,40},{40,48},{48,56},{56,64},{64,7... | collective-permute-start | bytes 98312 | tf_op jit(solution)/shard_map/while/body/eval_jaxpr/ppermute | solution.py:16
  222.0 8.4 %collective-permute-start = (bf16[1,128,128]{2,1,0:T(8,128)(2,1)S(1)}, bf16[1,128,128]{2,1,0:T(8,128)(2,1)S(1)}, u32[]{:S(2)}, u32[]{:S(2)}) collective-permute-start(bf16[1,128,128]{2,1,0:T(8,128)(2,1)S(1)} %fusion.74), channel_id=1, source_target_pairs={{0,8},{8,16},{16,24},{24,32},{32,40},{40,48},{48,56},{56,64},{64,7... | collective-permute-start | bytes 98312 | tf_op jit(solution)/shard_map/while/body/eval_jaxpr/ppermute | solution.py:16
  230.4 8.8 %collective-permute-start = (bf16[1,128,128]{2,1,0:T(8,128)(2,1)S(1)}, bf16[1,128,128]{2,1,0:T(8,128)(2,1)S(1)}, u32[]{:S(2)}, u32[]{:S(2)}) collective-permute-start(bf16[1,128,128]{2,1,0:T(8,128)(2,1)S(1)} %fusion.74), channel_id=1, source_target_pairs={{0,8},{8,16},{16,24},{24,32},{32,40},{40,48},{48,56},{56,64},{64,7... | collective-permute-start | bytes 98312 | tf_op jit(solution)/shard_map/while/body/eval_jaxpr/ppermute | solution.py:16
  239.2 8.7 %collective-permute-start = (bf16[1,128,128]{2,1,0:T(8,128)(2,1)S(1)}, bf16[1,128,128]{2,1,0:T(8,128)(2,1)S(1)}, u32[]{:S(2)}, u32[]{:S(2)}) collective-permute-start(bf16[1,128,128]{2,1,0:T(8,128)(2,1)S(1)} %fusion.74), channel_id=1, source_target_pairs={{0,8},{8,16},{16,24},{24,32},{32,40},{40,48},{48,56},{56,64},{64,7... | collective-permute-start | bytes 98312 | tf_op jit(solution)/shard_map/while/body/eval_jaxpr/ppermute | solution.py:16
  248.0 8.0 %collective-permute-start = (bf16[1,128,128]{2,1,0:T(8,128)(2,1)S(1)}, bf16[1,128,128]{2,1,0:T(8,128)(2,1)S(1)}, u32[]{:S(2)}, u32[]{:S(2)}) collective-permute-start(bf16[1,128,128]{2,1,0:T(8,128)(2,1)S(1)} %fusion.74), channel_id=1, source_target_pairs={{0,8},{8,16},{16,24},{24,32},{32,40},{40,48},{48,56},{56,64},{64,7... | collective-permute-start | bytes 98312 | tf_op jit(solution)/shard_map/while/body/eval_jaxpr/ppermute | solution.py:16
  256.0 9.1 %collective-permute-start = (bf16[1,128,128]{2,1,0:T(8,128)(2,1)S(1)}, bf16[1,128,128]{2,1,0:T(8,128)(2,1)S(1)}, u32[]{:S(2)}, u32[]{:S(2)}) collective-permute-start(bf16[1,128,128]{2,1,0:T(8,128)(2,1)S(1)} %fusion.74), channel_id=1, source_target_pairs={{0,8},{8,16},{16,24},{24,32},{32,40},{40,48},{48,56},{56,64},{64,7... | collective-permute-start | bytes 98312 | tf_op jit(solution)/shard_map/while/body/eval_jaxpr/ppermute | solution.py:16
  265.1 8.2 %collective-permute-start = (bf16[1,128,128]{2,1,0:T(8,128)(2,1)S(1)}, bf16[1,128,128]{2,1,0:T(8,128)(2,1)S(1)}, u32[]{:S(2)}, u32[]{:S(2)}) collective-permute-start(bf16[1,128,128]{2,1,0:T(8,128)(2,1)S(1)} %fusion.74), channel_id=1, source_target_pairs={{0,8},{8,16},{16,24},{24,32},{32,40},{40,48},{48,56},{56,64},{64,7... | collective-permute-start | bytes 98312 | tf_op jit(solution)/shard_map/while/body/eval_jaxpr/ppermute | solution.py:16
  273.4 7.8 %collective-permute-start = (bf16[1,128,128]{2,1,0:T(8,128)(2,1)S(1)}, bf16[1,128,128]{2,1,0:T(8,128)(2,1)S(1)}, u32[]{:S(2)}, u32[]{:S(2)}) collective-permute-start(bf16[1,128,128]{2,1,0:T(8,128)(2,1)S(1)} %fusion.74), channel_id=1, source_target_pairs={{0,8},{8,16},{16,24},{24,32},{32,40},{40,48},{48,56},{56,64},{64,7... | collective-permute-start | bytes 98312 | tf_op jit(solution)/shard_map/while/body/eval_jaxpr/ppermute | solution.py:16
  281.2 8.0 %collective-permute-start = (bf16[1,128,128]{2,1,0:T(8,128)(2,1)S(1)}, bf16[1,128,128]{2,1,0:T(8,128)(2,1)S(1)}, u32[]{:S(2)}, u32[]{:S(2)}) collective-permute-start(bf16[1,128,128]{2,1,0:T(8,128)(2,1)S(1)} %fusion.74), channel_id=1, source_target_pairs={{0,8},{8,16},{16,24},{24,32},{32,40},{40,48},{48,56},{56,64},{64,7... | collective-permute-start | bytes 98312 | tf_op jit(solution)/shard_map/while/body/eval_jaxpr/ppermute | solution.py:16
  289.3 8.6 %collective-permute-start = (bf16[1,128,128]{2,1,0:T(8,128)(2,1)S(1)}, bf16[1,128,128]{2,1,0:T(8,128)(2,1)S(1)}, u32[]{:S(2)}, u32[]{:S(2)}) collective-permute-start(bf16[1,128,128]{2,1,0:T(8,128)(2,1)S(1)} %fusion.74), channel_id=1, source_target_pairs={{0,8},{8,16},{16,24},{24,32},{32,40},{40,48},{48,56},{56,64},{64,7... | collective-permute-start | bytes 98312 | tf_op jit(solution)/shard_map/while/body/eval_jaxpr/ppermute | solution.py:16
  298.0 8.2 %collective-permute-start = (bf16[1,128,128]{2,1,0:T(8,128)(2,1)S(1)}, bf16[1,128,128]{2,1,0:T(8,128)(2,1)S(1)}, u32[]{:S(2)}, u32[]{:S(2)}) collective-permute-start(bf16[1,128,128]{2,1,0:T(8,128)(2,1)S(1)} %fusion.74), channel_id=1, source_target_pairs={{0,8},{8,16},{16,24},{24,32},{32,40},{40,48},{48,56},{56,64},{64,7... | collective-permute-start | bytes 98312 | tf_op jit(solution)/shard_map/while/body/eval_jaxpr/ppermute | solution.py:16
  306.2 8.4 %collective-permute-start = (bf16[1,128,128]{2,1,0:T(8,128)(2,1)S(1)}, bf16[1,128,128]{2,1,0:T(8,128)(2,1)S(1)}, u32[]{:S(2)}, u32[]{:S(2)}) collective-permute-start(bf16[1,128,128]{2,1,0:T(8,128)(2,1)S(1)} %fusion.74), channel_id=1, source_target_pairs={{0,8},{8,16},{16,24},{24,32},{32,40},{40,48},{48,56},{56,64},{64,7... | collective-permute-start | bytes 98312 | tf_op jit(solution)/shard_map/while/body/eval_jaxpr/ppermute | solution.py:16
  314.6 8.2 %collective-permute-start = (bf16[1,128,128]{2,1,0:T(8,128)(2,1)S(1)}, bf16[1,128,128]{2,1,0:T(8,128)(2,1)S(1)}, u32[]{:S(2)}, u32[]{:S(2)}) collective-permute-start(bf16[1,128,128]{2,1,0:T(8,128)(2,1)S(1)} %fusion.74), channel_id=1, source_target_pairs={{0,8},{8,16},{16,24},{24,32},{32,40},{40,48},{48,56},{56,64},{64,7... | collective-permute-start | bytes 98312 | tf_op jit(solution)/shard_map/while/body/eval_jaxpr/ppermute | solution.py:16
  322.9 8.3 %collective-permute-start = (bf16[1,128,128]{2,1,0:T(8,128)(2,1)S(1)}, bf16[1,128,128]{2,1,0:T(8,128)(2,1)S(1)}, u32[]{:S(2)}, u32[]{:S(2)}) collective-permute-start(bf16[1,128,128]{2,1,0:T(8,128)(2,1)S(1)} %fusion.74), channel_id=1, source_target_pairs={{0,8},{8,16},{16,24},{24,32},{32,40},{40,48},{48,56},{56,64},{64,7... | collective-permute-start | bytes 98312 | tf_op jit(solution)/shard_map/while/body/eval_jaxpr/ppermute | solution.py:16
  331.2 8.3 %collective-permute-start = (bf16[1,128,128]{2,1,0:T(8,128)(2,1)S(1)}, bf16[1,128,128]{2,1,0:T(8,128)(2,1)S(1)}, u32[]{:S(2)}, u32[]{:S(2)}) collective-permute-start(bf16[1,128,128]{2,1,0:T(8,128)(2,1)S(1)} %fusion.74), channel_id=1, source_target_pairs={{0,8},{8,16},{16,24},{24,32},{32,40},{40,48},{48,56},{56,64},{64,7... | collective-permute-start | bytes 98312 | tf_op jit(solution)/shard_map/while/body/eval_jaxpr/ppermute | solution.py:16
  339.6 8.3 %collective-permute-start = (bf16[1,128,128]{2,1,0:T(8,128)(2,1)S(1)}, bf16[1,128,128]{2,1,0:T(8,128)(2,1)S(1)}, u32[]{:S(2)}, u32[]{:S(2)}) collective-permute-start(bf16[1,128,128]{2,1,0:T(8,128)(2,1)S(1)} %fusion.74), channel_id=1, source_target_pairs={{0,8},{8,16},{16,24},{24,32},{32,40},{40,48},{48,56},{56,64},{64,7... | collective-permute-start | bytes 98312 | tf_op jit(solution)/shard_map/while/body/eval_jaxpr/ppermute | solution.py:16
  (43 other events, 1337.8 us)
Sparse Core Ops, SparseCore 0:
  9.9 77.1 all-gather.3
  89.7 81.8 all-gather.5
  174.1 82.8 all-gather.7
  379.8 97.9 reduce-scatter.1
